TPU v7x, 32 devices: a whole 2x2x4 slice. The times are simulated.
32 devices in a mesh: dp: 8 (over y, x, core), shard: 4 (over z).
Axes of the slice: x: 2, y: 2, z: 4, core: 2. Of those that a mesh axis runs over, the one named last changes fastest.
Arguments:
- gradients: bfloat16 [8, 44, 512, 512], P('dp', 'shard'), may hold values from -60 to 60
- owners: int32 [4, 11], P('shard'), may hold values from 0 to 7, as said below
- block_param: int32 [44], replicated, may hold values from 0 to 6, never falling along the last dimension, each value on 1 to 12 neighbouring positions
- left_stat: float32 [16, 4, 512, 512], P('dp', 'shard'), may hold values from -4 to 8, as said below
- right_stat: float32 [16, 4, 512, 512], P('dp', 'shard'), may hold values from -4 to 8, as said below
- moment: float32 [16, 4, 512, 512], P('dp', 'shard'), may hold values from 0.5 to 50
- left_root: bfloat16 [16, 4, 512, 512], P('dp', 'shard'), may hold values from -1 to 3.5, as said below
- right_root: bfloat16 [16, 4, 512, 512], P('dp', 'shard'), may hold values from -1 to 3.5, as said below
Outputs:
- new_left: float32 [16, 4, 512, 512], P('dp', 'shard')
- new_right: float32 [16, 4, 512, 512], P('dp', 'shard')
- new_moment: float32 [16, 4, 512, 512], P('dp', 'shard')
- update: bfloat16 [44, 512, 512], P('shard')
Inputs may be any that keep to these rules, and one draw needn't show every extreme that they name: `owners`: in each row, no value occurs more than 2 times, and some value occurs exactly 2 times. `left_stat`: each slot's matrix is symmetric. `right_stat`: each slot's matrix is symmetric. `left_root`: each slot's matrix is symmetric. `right_root`: each slot's matrix is symmetric.
All inputs are finite; a program needn't handle non-finite values.
Results may differ from a plain program's by a relative error of at most 0.0058.
Values may be sent and summed in bfloat16 or wider, within the bound.
No kernel may reach another device: no remote copies, remote signals or barrier semaphores. Data moves between devices by JAX's collectives and lax.ppermute only.
A program may use at most 192 MiB of HBM per device.

v0:
```python
import jax
import jax.numpy as jnp
from jax import lax
from jax.sharding import PartitionSpec as P

NPARAM = 7
decay_rate = 0.95
tiny_value = 1e-06


def on_device(gradients, owners, block_param, left_stat, right_stat, moment, left_root, right_root):
    replicas = lax.axis_size("dp")
    capacity = left_stat.shape[0]
    blocks = gradients.shape[1]
    block_width = gradients.shape[3]
    device = lax.axis_index("dp")
    column = lax.axis_index("shard")
    owner_row = owners[0]
    counter = jnp.arange(blocks, dtype=jnp.int32)
    same_owner = owner_row[:, None] == owner_row[None, :]
    earlier = counter[None, :] < counter[:, None]
    places = owner_row * capacity + jnp.sum(jnp.where(same_owner & earlier, 1, 0), axis=1).astype(
        jnp.int32
    )
    slot_ids = jnp.arange(replicas * capacity, dtype=jnp.int32)
    matches = places[None, :] == slot_ids[:, None]
    source = jnp.min(jnp.where(matches, counter[None, :], blocks), axis=1)
    partials = gradients[0].astype(jnp.float32)
    row_share = lax.psum_scatter(partials, "dp", scatter_dimension=1, tiled=True)
    share_padded = jnp.concatenate(
        [row_share, jnp.zeros((1,) + row_share.shape[1:], jnp.float32)], axis=0
    )
    outgoing = jnp.take(share_padded, source, axis=0).reshape(
        replicas, capacity, block_width // replicas, block_width
    )
    arrived = lax.all_to_all(outgoing, "dp", split_axis=0, concat_axis=2, tiled=True)
    summed = arrived[0]
    left_gram = jnp.einsum("cij,ckj->cik", summed, summed, precision=lax.Precision.HIGHEST)
    right_gram = jnp.einsum("cji,cjk->cik", summed, summed, precision=lax.Precision.HIGHEST)
    new_left = decay_rate * left_stat + (1.0 - decay_rate) * left_gram[:, None]
    new_right = decay_rate * right_stat + (1.0 - decay_rate) * right_gram[:, None]
    new_moment = decay_rate * moment + (1.0 - decay_rate) * (summed * summed)[:, None]
    adam_step = summed / (jnp.sqrt(new_moment[:, 0]) + tiny_value)
    left_half = jnp.einsum(
        "cij,cjk->cik",
        left_root[:, 0],
        summed.astype(jnp.bfloat16),
        preferred_element_type=jnp.float32,
    ).astype(jnp.bfloat16)
    direction = jnp.einsum(
        "cij,cjk->cik", left_half, right_root[:, 0], preferred_element_type=jnp.float32
    )
    my_slots = lax.dynamic_slice_in_dim(matches, device * capacity, capacity, 0)
    local_params = lax.dynamic_slice_in_dim(block_param, column * blocks, blocks, 0)
    slot_param = jnp.sum(jnp.where(my_slots, local_params[None, :], 0), axis=1)
    is_live = jnp.any(my_slots, axis=1)
    param_ids = jnp.arange(NPARAM, dtype=jnp.int32)
    member = (slot_param[:, None] == param_ids[None, :]) & is_live[:, None]
    adam_squares = jnp.sum(adam_step * adam_step, axis=(1, 2))
    direction_squares = jnp.sum(direction * direction, axis=(1, 2))
    adam_local = jnp.sum(jnp.where(member, adam_squares[:, None], 0.0), axis=0)
    direction_local = jnp.sum(jnp.where(member, direction_squares[:, None], 0.0), axis=0)
    adam_norm, direction_norm = lax.psum((adam_local, direction_local), ("dp", "shard"))
    graft_ratio = jnp.sqrt((adam_norm + tiny_value) / (direction_norm + tiny_value))
    slot_ratio = jnp.sum(jnp.where(member, graft_ratio[None, :], 0.0), axis=1)
    slot_update = (slot_ratio[:, None, None] * direction).astype(jnp.bfloat16)
    gathered = lax.all_gather(slot_update, "dp", axis=0, tiled=True)
    update = jnp.take(gathered, places, axis=0)
    return (new_left, new_right, new_moment, update)


def solution(mesh):
    return jax.shard_map(
        on_device,
        mesh=mesh,
        in_specs=(
            P("dp", "shard", None, None),
            P("shard", None),
            P(),
            P("dp", "shard", None, None),
            P("dp", "shard", None, None),
            P("dp", "shard", None, None),
            P("dp", "shard", None, None),
            P("dp", "shard", None, None),
        ),
        out_specs=(
            P("dp", "shard", None, None),
            P("dp", "shard", None, None),
            P("dp", "shard", None, None),
            P("shard", None, None),
        ),
        check_vma=False,
    )
```

profile of v0, /device:TPU:0, one launch (start us, length us, event | category | flops | bytes accessed | tf_op | source)
XLA Modules:
  0.0 273.2 jit_solution(2395701479978908789)
XLA Ops:
  7.2 0.0 copy-start
  7.2 0.0 reduce-scatter.2.cloned.1.call-start
  7.2 8.7 %bitcast_convert_fusion = f32[11,512,512]{2,1,0:T(8,128)} fusion(bf16[1,11,512,512]{3,2,1,0:T(8,128)(2,1)} %param.8), kind=kLoop, calls=%fused_computation.2 | loop fusion | flops 2883584 | bytes 17301504 | tf_op jit(solution)/shard_map/convert_element_type | solution.py:28
  15.9 0.0 copy-start.6
  15.9 0.0 reduce-scatter.2.cloned.1.call-update
  15.9 0.6 copy-done.6
  16.6 0.2 select_reduce_fusion.1
  16.7 0.1 select_reduce_fusion
  16.9 0.1 reduce_min.14
  17.0 88.7 %reduce-scatter.2.cloned.1.call-done = f32[11,64,512]{2,1,0:T(8,128)} async-done(((f32[11,512,512]{2,1,0:T(8,128)}), f32[11,64,512]{2,1,0:T(8,128)}) %reduce-scatter.2.cloned.1.call-update) | async-done | bytes 1441808 | tf_op jit(solution)/shard_map/reduce_scatter | solution.py:29
  105.6 1.5 concatenate.3
  107.2 2.0 gather_fusion
  109.2 3.3 %broadcast_select_fusion.1 = f32[8,2,64,512]{3,2,1,0:T(8,128)} fusion(f32[8,2,64,512]{3,2,1,0:T(8,128)} %bitcast.79, pred[8,2]{1,0:T(8,128)(4,1)S(1)} %compare_and_fusion), kind=kLoop, calls=%fused_computation.24 | loop fusion | flops 524288 | bytes 4194320 | tf_op jit(solution)/shard_map/jit(_take)/select_n | solution.py:33
  112.5 0.0 copy-start.5
  112.5 3.7 %all-to-all-start = ((f32[8,2,64,512]{3,2,1,0:T(8,128)}), f32[8,2,64,512]{3,2,1,0:T(8,128)S(1)}, u32[]{:S(2)}, u32[]{:S(2)}) async-start(f32[8,2,64,512]{3,2,1,0:T(8,128)} %broadcast_select_fusion.1), calls=%async_computation.1 | async-start | bytes 4194304 | tf_op jit(solution)/shard_map/all_to_all | solution.py:36
  116.2 0.0 all-gather.2.cloned.1.call-start
  116.3 0.0 copy-done.5
  116.3 0.1 dynamic_slice.7
  116.4 0.1 fusion.15
  116.5 0.1 select_reduce_fusion.5
  116.6 26.2 %all-to-all-done = f32[8,2,64,512]{3,2,1,0:T(8,128)S(1)} async-done(((f32[8,2,64,512]{3,2,1,0:T(8,128)}), f32[8,2,64,512]{3,2,1,0:T(8,128)S(1)}, u32[]{:S(2)}, u32[]{:S(2)}) %all-to-all-start) | async-done | bytes 2097184 | tf_op jit(solution)/shard_map/all_to_all | solution.py:36
  142.8 0.0 copy-start.2
  142.8 0.3 multiply_multiply_fusion
  143.1 1.1 copy-done.2
  144.1 0.2 copy.47
  144.3 0.0 copy-start.3
  144.3 2.0 copy.43
  146.3 0.2 copy-done.3
  146.6 2.8 %sqrt_add_fusion = (f32[2,1,512,512]{3,2,0,1:T(8,128)}, f32[2,1,512,512]{3,2,0,1:T(8,128)}) fusion(f32[1,2,8,64,512]{4,3,2,1,0:T(8,128)S(1)} %copy.47, f32[2,1,512,512]{3,2,1,0:T(8,128)S(1)} %copy-done.3), kind=kLoop, calls=%fused_computation.16 | loop fusion | flops 1572864 | bytes 8388608 | tf_op jit(solution)/shard_map/add | solution.py:43
  149.3 0.0 copy-done
  149.3 4.0 %multiply_reduce_fusion = (f32[2]{0:T(128)S(1)}, f32[2,512,512]{2,1,0:T(8,128)}) fusion(bf16[2,1,512,512]{3,2,1,0:T(8,128)(2,1)S(1)} %copy-done, bf16[2,1,512,512]{3,2,1,0:T(8,128)(2,1)} %param.14, f32[2,512,512]{2,1,0:T(8,128)S(1)} %bitcast.75), kind=kOutput, calls=%fused_computation.15 | convolution fusion | flops 1075838976 | bytes 6291464 | tf_op jit(solution)/shard_map/cij,cjk->cik/dot_general | solution.py:50
  153.3 2.7 fusion.3
  156.0 0.1 select_reduce_fusion.4
  156.1 39.5 %all-reduce.1 = (f32[7]{0:T(128)S(1)}, f32[7]{0:T(128)S(1)}) all-reduce(f32[7]{0:T(128)S(1)} %get-tuple-element.21, f32[7]{0:T(128)S(1)} %get-tuple-element.20), channel_id=1, replica_groups=mesh['dp'=8,'shard'=4] {'dp','shard'}, use_global_device_ids=true, to_apply=%region_10.11 | all-reduce | flops 14 | bytes 112 | tf_op jit(solution)/shard_map/psum | solution.py:63
  195.5 0.2 select_reduce_fusion.2
  195.7 3.0 %multiply_convert_fusion = bf16[2,512,512]{2,1,0:T(8,128)(2,1)} fusion(f32[2,512,512]{2,1,0:T(8,128)} %get-tuple-element.27, f32[2]{0:T(128)S(1)} %select_reduce_fusion.2), kind=kLoop, calls=%fused_computation.14 | loop fusion | flops 1048576 | bytes 3145736 | tf_op jit(solution)/shard_map/convert_element_type | solution.py:66
  198.7 0.0 all-gather.2.cloned.1.call-update
  198.8 0.0 copy-start.4
  198.8 6.1 %fusion = f32[2,1,512,512]{3,2,1,0:T(8,128)} fusion(f32[2,1,512,512]{3,2,1,0:T(8,128)} %param.12, f32[2,512,512]{2,1,0:T(8,128)S(1)} %bitcast.76), kind=kOutput, calls=%fused_computation.7 | convolution fusion | flops 3222798336 | bytes 6291456 | tf_op jit(solution)/shard_map/cji,cjk->cik/dot_general | solution.py:39
  204.9 0.0 copy-done.4
  204.9 5.0 %fusion.1 = f32[2,1,512,512]{3,2,1,0:T(8,128)} fusion(f32[2,1,512,512]{3,2,1,0:T(8,128)S(1)} %copy-done.4, f32[2,512,512]{2,1,0:T(8,128)S(1)} %bitcast.77), kind=kOutput, calls=%fused_computation.10 | convolution fusion | flops 3222798336 | bytes 6291456 | tf_op jit(solution)/shard_map/cij,ckj->cik/dot_general | solution.py:38
  209.9 43.1 %all-gather.2.cloned.1.call-done = bf16[16,512,512]{2,1,0:T(8,128)(2,1)} async-done(((bf16[2,512,512]{2,1,0:T(8,128)(2,1)}), bf16[16,512,512]{2,1,0:T(8,128)(2,1)}) %all-gather.2.cloned.1.call-update) | async-done | bytes 8388624 | tf_op jit(solution)/shard_map/all_gather | solution.py:67
  253.0 7.4 %gather_fusion.1 = bf16[11,512,512]{2,1,0:T(8,128)(2,1)} fusion(bf16[16,512,512]{2,1,0:T(8,128)(2,1)} %all-gather.2.cloned.1.call-done, s32[1024]{0:T(1024)S(1)} %pad_clamp_fusion), kind=kCustom, calls=%fused_computation.1 | custom fusion | bytes 11534380 | tf_op jit(solution)/shard_map/jit(_take)/gather | solution.py:68
  260.5 0.0 copy-start.1
  260.5 5.9 %broadcast_select_fusion = bf16[11,512,512]{2,1,0:T(8,128)(2,1)} fusion(bf16[11,512,512]{2,1,0:T(8,128)(2,1)} %gather_fusion.1, pred[11]{0:T(512)(128)(4,1)S(1)} %compare_and_fusion.2), kind=kLoop, calls=%fused_computation.3 | loop fusion | flops 2883584 | bytes 11534347 | tf_op jit(solution)/shard_map/jit(_take)/select_n | solution.py:68
  266.3 0.0 copy-done.1
  (9 shorter events, 0.1 us)
Async XLA Ops:
  7.2 142.2 %copy-start = (bf16[2,1,512,512]{3,2,1,0:T(8,128)(2,1)S(1)}, bf16[2,1,512,512]{3,2,1,0:T(8,128)(2,1)}, u32[]{:S(2)}) copy-start(bf16[2,1,512,512]{3,2,1,0:T(8,128)(2,1)} %param.15) | copy-start | bytes 3145732
  7.2 98.5 %reduce-scatter.2.cloned.1.call-start = ((), (), s32[]{:S(2)}) async-start(), calls=%async_computation.2 | async-start | bytes 12976128 | tf_op jit(solution)/shard_map/reduce_scatter | solution.py:29
  15.9 0.7 copy-start.6
  112.5 3.8 %copy-start.5 = (s32[44]{0:T(128)S(1)}, s32[44]{0:T(128)}, u32[]{:S(2)}) copy-start(s32[44]{0:T(128)} %param.10) | copy-start | bytes 532
  112.5 30.3 %all-to-all-start = ((f32[8,2,64,512]{3,2,1,0:T(8,128)}), f32[8,2,64,512]{3,2,1,0:T(8,128)S(1)}, u32[]{:S(2)}, u32[]{:S(2)}) async-start(f32[8,2,64,512]{3,2,1,0:T(8,128)} %broadcast_select_fusion.1), calls=%async_computation.1 | async-start | bytes 4194304 | tf_op jit(solution)/shard_map/all_to_all | solution.py:36
  116.2 136.8 %all-gather.2.cloned.1.call-start = ((), (), s32[]{:S(2)}) async-start(), calls=%async_computation.3 | async-start | bytes 9437184 | tf_op jit(solution)/shard_map/all_gather | solution.py:67
  142.8 1.3 copy-start.2
  144.3 2.2 copy-start.3
  198.8 6.2 %copy-start.4 = (f32[2,1,512,512]{3,2,1,0:T(8,128)S(1)}, f32[2,1,512,512]{3,2,1,0:T(8,128)}, u32[]{:S(2)}) copy-start(f32[2,1,512,512]{3,2,1,0:T(8,128)} %param.11) | copy-start | bytes 6291460
  260.5 5.9 %copy-start.1 = (bf16[2,1,512,512]{3,2,1,0:T(8,128)(2,1)S(1)}, bf16[2,1,512,512]{3,2,1,0:T(8,128)(2,1)}, u32[]{:S(2)}) copy-start(bf16[2,1,512,512]{3,2,1,0:T(8,128)(2,1)} %param.15) | copy-start | bytes 3145732
Sparse Core Ops, SparseCore 0:
  16.0 89.5 reduce-scatter.1
  198.9 54.1 all-gather.1
where the time goes:
time: 274 us; the launch traced here: 273 us
  waiting for transfers between devices  158 us (58%)
  blocking collectives  39.5 us (14%)
  other arithmetic  27.4 us (10%)
  local copies, waits for them, and re-layouts  15.3 us (6%)
  matrix products  15.1 us (6%)
  between operations  14.2 us (5%)
  starting transfers between devices  3.82 us (1%)
    reduce_scatter x1, waiting for transfers between devices, on_device(): lax.psum_scatter(partials, 'dp', scatter_dimension=1, tiled=True)  88.7 us
    all_gather x1, waiting for transfers between devices, on_device(): gathered = lax.all_gather(slot_update, 'dp', axis=0, tiled=True)  43.1 us
    psum x1, blocking collectives, on_device(): lax.psum((adam_local, direction_local), ('dp', 'shard'))  39.5 us
    all_to_all x1, waiting for transfers between devices, on_device(): lax.all_to_all(outgoing, 'dp', split_axis=0, concat_axis=2, tiled=True)  26.2 us
    convert_element_type x1, other arithmetic, on_device(): partials = gradients[0].astype(jnp.float32)  8.67 us
    gather x1, local copies, waits for them, and re-layouts, on_device(): update = jnp.take(gathered, places, axis=0)  7.44 us
    dot_general x1, matrix products, on_device(): jnp.einsum('cji,cjk->cik', summed, summed, precision=lax.Precision.HIGHEST)  6.14 us
    select_n x2, other arithmetic, on_device(): update = jnp.take(gathered, places, axis=0)  5.87 us
  transfers between devices with their start and end apart: 3, of which 3 were waited for; matrix products, arithmetic and copies ran while one was open for 4% of the time, Pallas kernels for 0%

commit v1 on v0

--- a/solution.py
+++ b/solution.py
@@ -33,7 +33,18 @@
     outgoing = jnp.take(share_padded, source, axis=0).reshape(
         replicas, capacity, block_width // replicas, block_width
     )
-    arrived = lax.all_to_all(outgoing, "dp", split_axis=0, concat_axis=2, tiled=True)
+    ways, here = (lax.axis_size("dp"), lax.axis_index("dp"))
+    width = outgoing.shape[0] // ways
+    lengths = list(outgoing.shape)
+    lengths[0] = width
+    height = lengths[2]
+    lengths[2] = height * ways
+    arrived = jnp.zeros(lengths, outgoing.dtype)
+    for mask in range(ways):
+        part = lax.dynamic_slice_in_dim(outgoing, (here ^ mask) * width, width, axis=0)
+        if mask:
+            part = lax.ppermute(part, "dp", [(d, d ^ mask) for d in range(ways)])
+        arrived = lax.dynamic_update_slice_in_dim(arrived, part, (here ^ mask) * height, axis=2)
     summed = arrived[0]
     left_gram = jnp.einsum("cij,ckj->cik", summed, summed, precision=lax.Precision.HIGHEST)
     right_gram = jnp.einsum("cji,cjk->cik", summed, summed, precision=lax.Precision.HIGHEST)

time: 274 us -> 265 us (0.967)
  waiting for transfers between devices: 158 us -> 150 us
    all_to_all x1 -> x0, waiting for transfers between devices: 26.2 us -> none  [on_device(): lax.all_to_all(outgoing, 'dp', split_axis=0, concat_axis=2, tiled=True)]
    ppermute x0 -> x7, waiting for transfers between devices: none -> 20.1 us  [on_device(): part = lax.ppermute(part, 'dp', [(d, d ^ mask) for d in range(ways)])]
    ppermute x0 -> x7, starting transfers between devices: none -> 5.19 us  [on_device(): part = lax.ppermute(part, 'dp', [(d, d ^ mask) for d in range(ways)])]
    all_to_all x1 -> x0, starting transfers between devices: 3.74 us -> none  [on_device(): lax.all_to_all(outgoing, 'dp', split_axis=0, concat_axis=2, tiled=True)]
    unnamed x0 -> x1, other arithmetic: none -> 3.58 us
    add x1 -> x0, other arithmetic: 2.78 us -> none  [on_device(): adam_step = summed / (jnp.sqrt(new_moment[:, 0]) + tiny_value)]
  transfers between devices with their start and end apart: 3 -> 9, of which waited for: 3 -> 5; matrix products, arithmetic and copies ran while one was open for 4% -> 6% of each run, Pallas kernels for 0% -> 0%
where the time goes in v1:
time: 265 us; the launch traced here: 264 us
  waiting for transfers between devices  150 us (57%)
  blocking collectives  39.5 us (15%)
  other arithmetic  25 us (9%)
  local copies, waits for them, and re-layouts  15.8 us (6%)
  between operations  14.4 us (5%)
  matrix products  14 us (5%)
  starting transfers between devices  5.27 us (2%)
    reduce_scatter x1, waiting for transfers between devices, on_device(): lax.psum_scatter(partials, 'dp', scatter_dimension=1, tiled=True)  88.7 us
    all_gather x1, waiting for transfers between devices, on_device(): gathered = lax.all_gather(slot_update, 'dp', axis=0, tiled=True)  41.5 us
    psum x1, blocking collectives, on_device(): lax.psum((adam_local, direction_local), ('dp', 'shard'))  39.5 us
    ppermute x7, waiting for transfers between devices, on_device(): part = lax.ppermute(part, 'dp', [(d, d ^ mask) for d in range(ways)])  20.1 us
    convert_element_type x1, other arithmetic, on_device(): partials = gradients[0].astype(jnp.float32)  8.67 us
    gather x1, local copies, waits for them, and re-layouts, on_device(): update = jnp.take(gathered, places, axis=0)  7.44 us
    select_n x2, other arithmetic, on_device(): update = jnp.take(gathered, places, axis=0)  5.87 us
  transfers between devices with their start and end apart: 9, of which 5 were waited for; matrix products, arithmetic and copies ran while one was open for 6% of the time, Pallas kernels for 0%

profile of v1, /device:TPU:0, one launch (start us, length us, event | category | flops | bytes accessed | tf_op | source)
XLA Modules:
  0.0 264.3 jit_solution(6561988839351269895)
XLA Ops:
  7.2 0.0 copy-start
  7.2 0.0 reduce-scatter.2.cloned.1.call-start
  7.2 8.7 %bitcast_convert_fusion = f32[11,512,512]{2,1,0:T(8,128)} fusion(bf16[1,11,512,512]{3,2,1,0:T(8,128)(2,1)} %param.8), kind=kLoop, calls=%fused_computation.2 | loop fusion | flops 2883584 | bytes 17301504 | tf_op jit(solution)/shard_map/convert_element_type | solution.py:28
  15.9 0.0 copy-start.9
  15.9 0.0 reduce-scatter.2.cloned.1.call-update
  15.9 0.0 all-gather.2.cloned.1.call-start
  16.0 0.5 copy-done.9
  16.6 0.2 select_reduce_fusion.1
  16.7 0.1 select_reduce_fusion
  16.9 0.1 reduce_min.14
  17.0 88.7 %reduce-scatter.2.cloned.1.call-done = f32[11,64,512]{2,1,0:T(8,128)} async-done(((f32[11,512,512]{2,1,0:T(8,128)}), f32[11,64,512]{2,1,0:T(8,128)}) %reduce-scatter.2.cloned.1.call-update) | async-done | bytes 1441808 | tf_op jit(solution)/shard_map/reduce_scatter | solution.py:29
  105.6 1.5 concatenate.3
  107.2 2.0 gather_fusion
  109.2 1.9 broadcast_select_fusion.1
  111.1 0.0 copy-start.3
  111.1 1.3 copy-done.3
  112.4 0.0 copy-start.8
  112.4 1.2 constant_dynamic-slice_fusion.1
  113.7 0.0 collective-permute-start
  113.8 0.0 copy-done.8
  113.8 0.0 copy-start.7
  113.8 0.0 copy-start.6
  113.8 0.1 dynamic_slice.39
  113.9 0.1 fusion.16
  114.0 0.1 select_reduce_fusion.5
  114.1 1.5 collective-permute-start.1
  115.7 0.3 collective-permute-start.2
  116.0 1.5 collective-permute-start.3
  117.5 0.2 collective-permute-start.4
  117.7 0.2 squeeze.28
  117.9 0.0 copy-start.2
  117.9 1.1 bitcast_dynamic-update-slice_fusion.7
  119.1 0.0 collective-permute-done
  119.1 0.0 copy-done.7
  119.1 1.5 collective-permute-start.5
  120.6 2.9 %collective-permute-done.1 = f32[1,2,64,512]{3,2,1,0:T(8,128)S(1)} collective-permute-done((f32[1,2,64,512]{3,2,1,0:T(8,128)}, f32[1,2,64,512]{3,2,1,0:T(8,128)S(1)}, u32[]{:S(2)}, u32[]{:S(2)}) %collective-permute-start.1) | collective-permute-done | bytes 262176 | tf_op jit(solution)/shard_map/ppermute | solution.py:46
  123.6 0.0 copy-done.6
  123.6 0.1 collective-permute-start.6
  123.7 4.6 %collective-permute-done.2 = f32[1,2,64,512]{3,2,1,0:T(8,128)S(1)} collective-permute-done((f32[1,2,64,512]{3,2,1,0:T(8,128)}, f32[1,2,64,512]{3,2,1,0:T(8,128)S(1)}, u32[]{:S(2)}, u32[]{:S(2)}) %collective-permute-start.2) | collective-permute-done | bytes 262176 | tf_op jit(solution)/shard_map/ppermute | solution.py:46
  128.3 0.0 collective-permute-done.3
  128.4 12.6 %collective-permute-done.4 = f32[1,2,64,512]{3,2,1,0:T(8,128)S(1)} collective-permute-done((f32[1,2,64,512]{3,2,1,0:T(8,128)}, f32[1,2,64,512]{3,2,1,0:T(8,128)S(1)}, u32[]{:S(2)}, u32[]{:S(2)}) %collective-permute-start.4) | collective-permute-done | bytes 262176 | tf_op jit(solution)/shard_map/ppermute | solution.py:46
  141.0 0.0 collective-permute-done.5
  141.0 0.0 collective-permute-done.6
  141.1 0.0 copy-done.2
  141.1 1.2 fusion.3
  142.3 0.0 copy-done
  142.3 4.0 %multiply_reduce_fusion = (f32[2]{0:T(128)S(1)}, f32[2,512,512]{2,1,0:T(8,128)}) fusion(bf16[2,1,512,512]{3,2,1,0:T(8,128)(2,1)S(1)} %copy-done, bf16[2,1,512,512]{3,2,1,0:T(8,128)(2,1)} %param.14, f32[2,512,512]{2,1,0:T(8,128)S(1)} %bitcast_dynamic-update-slice_fusion), kind=kOutput, calls=%fused_computation.15 | convolution fusion | flops 1075838976 | bytes 6291464 | tf_op jit(solution)/shard_map/cij,cjk->cik/dot_general | solution.py:61
  146.3 0.1 select_reduce_fusion.4
  146.4 39.5 %all-reduce.1 = (f32[7]{0:T(128)S(1)}, f32[7]{0:T(128)S(1)}) all-reduce(f32[7]{0:T(128)S(1)} %get-tuple-element.21, f32[7]{0:T(128)S(1)} %get-tuple-element.20), channel_id=1, replica_groups=mesh['dp'=8,'shard'=4] {'dp','shard'}, use_global_device_ids=true, to_apply=%region_10.11 | all-reduce | flops 14 | bytes 112 | tf_op jit(solution)/shard_map/psum | solution.py:74
  185.9 0.2 select_reduce_fusion.2
  186.1 2.9 %multiply_convert_fusion = bf16[2,512,512]{2,1,0:T(8,128)(2,1)} fusion(f32[2,512,512]{2,1,0:T(8,128)} %get-tuple-element.32, f32[2]{0:T(128)S(1)} %select_reduce_fusion.2), kind=kLoop, calls=%fused_computation.14 | loop fusion | flops 1048576 | bytes 3145736 | tf_op jit(solution)/shard_map/convert_element_type | solution.py:77
  189.0 0.0 all-gather.2.cloned.1.call-update
  189.0 0.0 copy-start.4
  189.0 3.6 %fusion.4 = f32[2,1,512,512]{3,2,1,0:T(8,128)} fusion(f32[2,512,512]{2,1,0:T(8,128)S(1)} %bitcast_dynamic-update-slice_fusion, f32[2,1,512,512]{3,2,1,0:T(8,128)} %param.13), kind=kLoop, calls=%fused_computation.17 | loop fusion | flops 2097152 | bytes 6291456
  192.6 0.0 copy-done.4
  192.6 0.0 copy-start.5
  192.6 5.0 %fusion.1 = f32[2,1,512,512]{3,2,1,0:T(8,128)} fusion(f32[2,1,512,512]{3,2,1,0:T(8,128)S(1)} %copy-done.4, f32[2,512,512]{2,1,0:T(8,128)S(1)} %bitcast_dynamic-update-slice_fusion), kind=kOutput, calls=%fused_computation.9 | convolution fusion | flops 3222798336 | bytes 6291456 | tf_op jit(solution)/shard_map/cji,cjk->cik/dot_general | solution.py:50
  197.6 0.0 copy-done.5
  197.6 5.0 %fusion.2 = f32[2,1,512,512]{3,2,1,0:T(8,128)} fusion(f32[2,1,512,512]{3,2,1,0:T(8,128)S(1)} %copy-done.5, f32[2,512,512]{2,1,0:T(8,128)S(1)} %bitcast_dynamic-update-slice_fusion), kind=kOutput, calls=%fused_computation.12 | convolution fusion | flops 3222798336 | bytes 6291456 | tf_op jit(solution)/shard_map/cij,ckj->cik/dot_general | solution.py:49
  202.6 41.5 %all-gather.2.cloned.1.call-done = bf16[16,512,512]{2,1,0:T(8,128)(2,1)} async-done(((bf16[2,512,512]{2,1,0:T(8,128)(2,1)}), bf16[16,512,512]{2,1,0:T(8,128)(2,1)}) %all-gather.2.cloned.1.call-update) | async-done | bytes 8388624 | tf_op jit(solution)/shard_map/all_gather | solution.py:78
  244.1 7.4 %gather_fusion.1 = bf16[11,512,512]{2,1,0:T(8,128)(2,1)} fusion(bf16[16,512,512]{2,1,0:T(8,128)(2,1)} %all-gather.2.cloned.1.call-done, s32[1024]{0:T(1024)S(1)} %pad_clamp_fusion), kind=kCustom, calls=%fused_computation.1 | custom fusion | bytes 11534380 | tf_op jit(solution)/shard_map/jit(_take)/gather | solution.py:79
  251.6 0.0 copy-start.1
  251.6 5.9 %broadcast_select_fusion = bf16[11,512,512]{2,1,0:T(8,128)(2,1)} fusion(bf16[11,512,512]{2,1,0:T(8,128)(2,1)} %gather_fusion.1, pred[11]{0:T(512)(128)(4,1)S(1)} %compare_and_fusion.2), kind=kLoop, calls=%fused_computation.3 | loop fusion | flops 2883584 | bytes 11534347 | tf_op jit(solution)/shard_map/jit(_take)/select_n | solution.py:79
  257.4 0.0 copy-done.1
  (16 shorter events, 0.2 us)
Async XLA Ops:
  7.2 135.1 %copy-start = (bf16[2,1,512,512]{3,2,1,0:T(8,128)(2,1)S(1)}, bf16[2,1,512,512]{3,2,1,0:T(8,128)(2,1)}, u32[]{:S(2)}) copy-start(bf16[2,1,512,512]{3,2,1,0:T(8,128)(2,1)} %param.15) | copy-start | bytes 3145732
  7.2 98.5 %reduce-scatter.2.cloned.1.call-start = ((), (), s32[]{:S(2)}) async-start(), calls=%async_computation.1 | async-start | bytes 12976128 | tf_op jit(solution)/shard_map/reduce_scatter | solution.py:29
  15.9 0.7 copy-start.9
  15.9 228.2 %all-gather.2.cloned.1.call-start = ((), (), s32[]{:S(2)}) async-start(), calls=%async_computation.2 | async-start | bytes 9437184 | tf_op jit(solution)/shard_map/all_gather | solution.py:78
  111.1 1.3 copy-start.3
  112.4 1.3 copy-start.8
  113.7 5.4 %collective-permute-start = (f32[1,2,64,512]{3,2,1,0:T(8,128)}, f32[1,2,64,512]{3,2,1,0:T(8,128)S(1)}, u32[]{:S(2)}, u32[]{:S(2)}) collective-permute-start(f32[1,2,64,512]{3,2,1,0:T(8,128)} %get-tuple-element.30), channel_id=1, source_target_pairs={{0,4},{4,0},{8,12},{12,8},{16,20},{20,16},{24,28},{28,24},{1,5},{5... | collective-permute-start | bytes 786440 | tf_op jit(solution)/shard_map/ppermute | solution.py:46
  113.8 5.3 %copy-start.7 = (f32[1,2,64,512]{3,2,1,0:T(8,128)S(1)}, f32[1,2,64,512]{3,2,1,0:T(8,128)}, u32[]{:S(2)}) copy-start(f32[1,2,64,512]{3,2,1,0:T(8,128)} %get-tuple-element.25) | copy-start | bytes 786436
  113.8 9.8 %copy-start.6 = (f32[1,2,64,512]{3,2,1,0:T(8,128)S(1)}, f32[1,2,64,512]{3,2,1,0:T(8,128)}, u32[]{:S(2)}) copy-start(f32[1,2,64,512]{3,2,1,0:T(8,128)} %get-tuple-element.24) | copy-start | bytes 786436
  114.1 9.5 %collective-permute-start.1 = (f32[1,2,64,512]{3,2,1,0:T(8,128)}, f32[1,2,64,512]{3,2,1,0:T(8,128)S(1)}, u32[]{:S(2)}, u32[]{:S(2)}) collective-permute-start(f32[1,2,64,512]{3,2,1,0:T(8,128)} %get-tuple-element.29), channel_id=1, source_target_pairs={{0,8},{4,12},{8,0},{12,4},{16,24},{20,28},{24,16},{28,20},{1,9},{5... | collective-permute-start | bytes 786440 | tf_op jit(solution)/shard_map/ppermute | solution.py:46
  115.7 12.6 %collective-permute-start.2 = (f32[1,2,64,512]{3,2,1,0:T(8,128)}, f32[1,2,64,512]{3,2,1,0:T(8,128)S(1)}, u32[]{:S(2)}, u32[]{:S(2)}) collective-permute-start(f32[1,2,64,512]{3,2,1,0:T(8,128)} %get-tuple-element.28), channel_id=1, source_target_pairs={{0,12},{4,8},{8,4},{12,0},{16,28},{20,24},{24,20},{28,16},{1,13},{... | collective-permute-start | bytes 786440 | tf_op jit(solution)/shard_map/ppermute | solution.py:46
  116.0 12.4 %collective-permute-start.3 = (f32[1,2,64,512]{3,2,1,0:T(8,128)}, f32[1,2,64,512]{3,2,1,0:T(8,128)S(1)}, u32[]{:S(2)}, u32[]{:S(2)}) collective-permute-start(f32[1,2,64,512]{3,2,1,0:T(8,128)} %get-tuple-element.27), channel_id=1, source_target_pairs={{0,16},{4,20},{8,24},{12,28},{16,0},{20,4},{24,8},{28,12},{1,17},{... | collective-permute-start | bytes 786440 | tf_op jit(solution)/shard_map/ppermute | solution.py:46
  117.5 23.5 %collective-permute-start.4 = (f32[1,2,64,512]{3,2,1,0:T(8,128)}, f32[1,2,64,512]{3,2,1,0:T(8,128)S(1)}, u32[]{:S(2)}, u32[]{:S(2)}) collective-permute-start(f32[1,2,64,512]{3,2,1,0:T(8,128)} %get-tuple-element.26), channel_id=1, source_target_pairs={{0,20},{4,16},{8,28},{12,24},{16,4},{20,0},{24,12},{28,8},{1,21},{... | collective-permute-start | bytes 786440 | tf_op jit(solution)/shard_map/ppermute | solution.py:46
  117.9 23.2 %copy-start.2 = (f32[2,1,512,512]{3,2,1,0:T(8,128)S(1)}, f32[2,1,512,512]{3,2,1,0:T(8,128)}, u32[]{:S(2)}) copy-start(f32[2,1,512,512]{3,2,1,0:T(8,128)} %param.13) | copy-start | bytes 6291460
  119.1 21.9 %collective-permute-start.5 = (f32[1,2,64,512]{3,2,1,0:T(8,128)S(1)}, f32[1,2,64,512]{3,2,1,0:T(8,128)S(1)}, u32[]{:S(2)}, u32[]{:S(2)}) collective-permute-start(f32[1,2,64,512]{3,2,1,0:T(8,128)S(1)} %copy-done.7), channel_id=1, source_target_pairs={{0,24},{4,28},{8,16},{12,20},{16,8},{20,12},{24,0},{28,4},{1,25},{... | collective-permute-start | bytes 786440 | tf_op jit(solution)/shard_map/ppermute | solution.py:46
  123.6 17.5 %collective-permute-start.6 = (f32[1,2,64,512]{3,2,1,0:T(8,128)S(1)}, f32[1,2,64,512]{3,2,1,0:T(8,128)S(1)}, u32[]{:S(2)}, u32[]{:S(2)}) collective-permute-start(f32[1,2,64,512]{3,2,1,0:T(8,128)S(1)} %copy-done.6), channel_id=1, source_target_pairs={{0,28},{4,24},{8,20},{12,16},{16,12},{20,8},{24,4},{28,0},{1,29},{... | collective-permute-start | bytes 786440 | tf_op jit(solution)/shard_map/ppermute | solution.py:46
  189.0 3.6 %copy-start.4 = (f32[2,1,512,512]{3,2,1,0:T(8,128)S(1)}, f32[2,1,512,512]{3,2,1,0:T(8,128)}, u32[]{:S(2)}) copy-start(f32[2,1,512,512]{3,2,1,0:T(8,128)} %param.12) | copy-start | bytes 6291460
  192.6 5.0 %copy-start.5 = (f32[2,1,512,512]{3,2,1,0:T(8,128)S(1)}, f32[2,1,512,512]{3,2,1,0:T(8,128)}, u32[]{:S(2)}) copy-start(f32[2,1,512,512]{3,2,1,0:T(8,128)} %param.11) | copy-start | bytes 6291460
  251.6 5.9 %copy-start.1 = (bf16[2,1,512,512]{3,2,1,0:T(8,128)(2,1)S(1)}, bf16[2,1,512,512]{3,2,1,0:T(8,128)(2,1)}, u32[]{:S(2)}) copy-start(bf16[2,1,512,512]{3,2,1,0:T(8,128)(2,1)} %param.15) | copy-start | bytes 3145732
Sparse Core Ops, SparseCore 0:
  16.0 89.5 reduce-scatter.1
  189.1 54.9 all-gather.1
